TPU v7x, 256 devices: a whole 4x4x8 slice. The times are simulated.
256 devices in a mesh: layer: 4 (over y), row: 16 (over z, core), col: 4 (over x).
Axes of the slice: x: 4, y: 4, z: 8, core: 2. Of those that a mesh axis runs over, the one named last changes fastest.
Arguments:
- ancestor: float32 [6144, 6144], P('row', 'col'), may hold values from -6 to 6
- leaf_lower: bfloat16 [4, 8, 6144, 512], P('layer', 'col', 'row'), may hold values from -6 to 6
- leaf_upper: bfloat16 [4, 8, 512, 6144], P('layer', None, 'row', 'col'), may hold values from -6 to 6
- leaf_upper_inv: bfloat16 [4, 8, 512, 512], P('layer', 'col'), may hold values from -1 to 1, as said below
- leaf_lower_inv: bfloat16 [4, 8, 512, 512], P('layer'), may hold values from -1 to 2, as said below
- leaf_pivots: int32 [4, 8, 512], P('layer'), may hold values from 0 to 511, each once within a row
- leaf_tiles: int32 [4, 8, 24, 24], P('layer'), may hold values 0 or 1
- anc_upper_inv: bfloat16 [512, 512], replicated, may hold values from -1 to 1, as said below
- anc_lower_inv: bfloat16 [512, 512], replicated, may hold values from -1 to 2, as said below
- anc_pivots: int32 [512], replicated, may hold values from 0 to 511, each once
- anc_tiles: int32 [24, 24], replicated, may hold values 0 or 1
Outputs:
- anc_lower: bfloat16 [6144, 512], P('row')
- anc_upper: bfloat16 [512, 6144], P(None, 'col')
- schur: float32 [6144, 6144], P('row', 'col')
Inputs may be any that keep to these rules, and one draw needn't show every extreme that they name: leaf_upper_inv[l,k] is upper triangular with positive diagonal. leaf_lower_inv[l,k] is lower triangular with positive diagonal. `anc_upper_inv`: upper triangular with positive diagonal. `anc_lower_inv`: lower triangular with positive diagonal.
All inputs are finite; a program needn't handle non-finite values. No bound on the sum of `leaf_tiles` on one device may be relied on, other than what follows from the above.
Results may differ from a plain program's by a relative error of at most 0.0085.
Values may be sent and summed in bfloat16 or wider, within the bound.
A program may use at most 128 MiB of HBM per device.

v0:
```python
import jax
import jax.numpy as jnp
from jax import lax
from jax.sharding import PartitionSpec as P

W = 512
TB = 256
NT = 24


def joined_along(blocks, dim):
    blocks = jnp.moveaxis(blocks, 0, dim)
    lengths = blocks.shape
    return blocks.reshape(*lengths[:dim], lengths[dim] * lengths[dim + 1], *lengths[dim + 2 :])


def sent_to_all(x, axis):
    count = lax.axis_size(axis)
    return lax.all_to_all(jnp.broadcast_to(x[None], (count, *x.shape)), axis, 0, 0, tiled=True)


def gathered_copies(x, axis, dim):
    return joined_along(sent_to_all(x, axis), dim)


def from_root(x, axis, root):
    return lax.dynamic_index_in_dim(lax.all_gather(x, axis), root, 0, keepdims=False)


def onehot_tiles(first, count):
    positions = first + jnp.arange(count, dtype=jnp.int32)
    tile_index = positions // TB
    return (tile_index[:, None] == jnp.arange(NT, dtype=jnp.int32)[None, :]).astype(jnp.float32)


def shards(
    ancestor,
    leaf_lower,
    leaf_upper,
    leaf_upper_inv,
    leaf_lower_inv,
    leaf_pivots,
    leaf_tiles,
    anc_upper_inv,
    anc_lower_inv,
    anc_pivots,
    anc_tiles,
):
    row_count, col_count = ancestor.shape
    panel_rows = leaf_upper.shape[2]
    row_onehot = onehot_tiles(lax.axis_index("row") * row_count, row_count)
    col_onehot = onehot_tiles(lax.axis_index("col") * col_count, col_count)
    upper_local = leaf_upper[0]
    column_share = lax.all_to_all(upper_local, "row", split_axis=2, concat_axis=1, tiled=True)
    permuted = jnp.take_along_axis(column_share, leaf_pivots[0][:, :, None], axis=1)
    finished = jnp.einsum(
        "kij,kjc->kic", leaf_lower_inv[0], permuted, preferred_element_type=jnp.float32
    ).astype(jnp.bfloat16)
    upper_all = lax.all_gather(finished, "row", axis=2, tiled=True)
    own_lower = jnp.einsum(
        "jrw,jwv->jrv", leaf_lower[0], leaf_upper_inv[0], preferred_element_type=jnp.float32
    ).astype(jnp.bfloat16)
    tiles_float = leaf_tiles[0].astype(jnp.float32)
    masks = jnp.einsum("rt,mts,cs->mrc", row_onehot, tiles_float, col_onehot)
    products = jnp.einsum(
        "mrw,mwc->mrc",
        lax.all_gather(own_lower, "col", axis=0, tiled=True),
        upper_all,
        preferred_element_type=jnp.float32,
    )
    contrib = jnp.sum(masks * products, axis=0)
    total = lax.psum(contrib, "layer")
    a_sum = ancestor + total
    local_pivot = a_sum[:panel_rows].astype(jnp.bfloat16)
    gathered = gathered_copies(local_pivot, "row", 0)
    reordered = jnp.take(gathered, anc_pivots, axis=0)
    anc_upper = jnp.dot(anc_lower_inv, reordered, preferred_element_type=jnp.float32).astype(
        jnp.bfloat16
    )
    columns = a_sum[:, :W].astype(jnp.bfloat16)
    panel = jnp.dot(columns, anc_upper_inv, preferred_element_type=jnp.float32).astype(jnp.bfloat16)
    anc_lower = from_root(panel, "col", 0)
    anc_mask = jnp.einsum("rt,ts,cs->rc", row_onehot, anc_tiles.astype(jnp.float32), col_onehot)
    schur = a_sum - anc_mask * jnp.dot(anc_lower, anc_upper, preferred_element_type=jnp.float32)
    return (anc_lower, anc_upper, schur)


def solution(mesh):
    return jax.shard_map(
        shards,
        mesh=mesh,
        in_specs=(
            P("row", "col"),
            P("layer", "col", "row", None),
            P("layer", None, "row", "col"),
            P("layer", "col", None, None),
            P("layer", None, None, None),
            P("layer", None, None),
            P("layer", None, None, None),
            P(),
            P(),
            P(),
            P(),
        ),
        out_specs=(P("row", None), P(None, "col"), P("row", "col")),
        check_vma=False,
    )
```

profile of v0, /device:TPU:1, one launch (start us, length us, event | category | flops | bytes accessed | tf_op | source)
XLA Modules:
  0.0 328.2 jit_solution(1591160123530114196)
XLA Ops:
  7.2 0.0 copy-start
  7.2 0.0 copy-start.6
  7.2 0.0 all-gather.5.cloned.1.call-start
  7.2 1.2 copy-done
  8.4 2.6 convolution_convert_fusion.1
  11.0 0.0 all-gather.5.cloned.1.call-update
  11.0 0.0 copy-done.6
  11.0 3.5 %copy.16 = bf16[1,8,32,1536]{2,1,3,0:T(8,128)(2,1)} copy(bf16[1,8,32,1536]{3,2,1,0:T(8,128)(2,1)S(1)} %copy-done.6) | data formatting | bytes 1572864 | tf_op args[2]
  14.5 3.1 bitcast_bitcast_fusion
  17.6 5.7 %reshape.121 = bf16[16,2,12288]{2,1,0:T(2,128)(2,1)} reshape(bf16[1536,8,32]{2,1,0:T(8,128)(2,1)} %bitcast_bitcast_fusion) | data formatting | bytes 1572864
  23.3 10.0 %all-to-all-start = ((bf16[16,2,12288]{2,1,0:T(2,128)(2,1)}), bf16[16,2,12288]{2,1,0:T(2,128)(2,1)S(1)}, u32[]{:S(2)}, u32[]{:S(2)}) async-start(bf16[16,2,12288]{2,1,0:T(2,128)(2,1)} %reshape.121), calls=%async_computation | async-start | bytes 1572864 | tf_op jit(solution)/shard_map/all_to_all | solution.py:54
  33.3 0.0 all-gather.7.cloned.1.call-start
  33.4 22.6 %all-to-all-done = bf16[16,2,12288]{2,1,0:T(2,128)(2,1)S(1)} async-done(((bf16[16,2,12288]{2,1,0:T(2,128)(2,1)}), bf16[16,2,12288]{2,1,0:T(2,128)(2,1)S(1)}, u32[]{:S(2)}, u32[]{:S(2)}) %all-to-all-start) | async-done | bytes 786464 | tf_op jit(solution)/shard_map/all_to_all | solution.py:54
  56.0 2.7 reshape.122
  58.7 3.9 %copy.17 = bf16[8,32,16,96]{3,1,2,0:T(8,128)(2,1)S(1)} copy(bf16[8,32,16,96]{1,0,3,2:T(8,128)(2,1)} %bitcast.62) | data formatting | bytes 1572864 | tf_op jit(solution)/shard_map/all_to_all | solution.py:54
  62.6 21.7 %gather_fusion.1 = bf16[4096,96]{1,0:T(8,128)(2,1)S(1)} fusion(bf16[8,512,96]{2,1,0:T(8,128)(2,1)S(1)} %bitcast.61, s32[4096]{0:T(1024)S(1)} %bitcast.59), kind=kCustom, calls=%fused_computation.1 | custom fusion | bytes 1605632 | tf_op jit(solution)/shard_map/jit(take_along_axis)/gather | solution.py:55
  84.3 4.5 %fusion.8 = bf16[8,512,96]{1,2,0:T(8,128)(2,1)} fusion(bf16[1,8,512,512]{3,2,1,0:T(8,128)(2,1)} %param.15, bf16[8,512,96]{2,1,0:T(8,128)(2,1)S(1)} %bitcast.64, pred[8,512]{1,0:T(8,128)(4,1)S(1)} %compare_and_fusion), kind=kOutput, calls=%fused_computation.12 | convolution fusion | flops 403439616 | bytes 5771264 | tf_op jit(solution)/shard_map/kij,kjc->kic/dot_general | solution.py:56
  88.8 0.0 all-gather.7.cloned.1.call-update
  88.8 0.0 all-reduce.2.cloned.1.call-start
  88.9 0.0 copy-start.7
  88.9 0.0 all-gather.5.cloned.1.call-done
  88.9 72.9 %all-gather.7.cloned.1.call-done = bf16[8,512,1536]{1,2,0:T(8,128)(2,1)} async-done(((bf16[8,512,96]{1,2,0:T(8,128)(2,1)}), bf16[8,512,1536]{1,2,0:T(8,128)(2,1)}) %all-gather.7.cloned.1.call-update) | async-done | bytes 12582928 | tf_op jit(solution)/shard_map/all_gather | solution.py:59
  161.8 17.2 %fusion.50 = f32[8,384,1536]{2,1,0:T(8,128)} fusion(bf16[8,384,512]{2,1,0:T(8,128)(2,1)} %all-gather.5.cloned.1.call-done, bf16[8,512,1536]{1,2,0:T(8,128)(2,1)} %all-gather.7.cloned.1.call-done), kind=kOutput, calls=%fused_computation.66 | convolution fusion | flops 4831838208 | bytes 34603008 | tf_op jit(solution)/shard_map/mrw,mwc->mrc/dot_general | solution.py:65
  179.1 9.6 %multiply_reduce_fusion = f32[384,1536]{1,0:T(8,128)} fusion(f32[8,384,1536]{2,1,0:T(8,128)} %fusion.50, s32[1,8,24,24]{3,2,1,0:T(8,128)S(1)} %copy-done.7, s32[384]{0:T(512)S(1)} %add_select_fusion.1, s32[1536]{0:T(1024)S(1)} %add_select_fusion), kind=kOutput, calls=%fused_computation.2 | convolution fusion | flops 238929408 | bytes 21259776 | tf_op jit(solution)/shard_map/rt,mts,cs->mrc/dot_general | solution.py:64
  188.7 0.0 all-reduce.2.cloned.1.call-update
  188.7 66.2 %all-reduce.2.cloned.1.call-done = f32[384,1536]{1,0:T(8,128)} async-done(((f32[384,1536]{1,0:T(8,128)}), f32[384,1536]{1,0:T(8,128)}) %all-reduce.2.cloned.1.call-update) | async-done | bytes 2359312 | tf_op jit(solution)/shard_map/psum | solution.py:72
  254.9 0.0 copy-done.3
  254.9 3.6 %fusion.49 = (bf16[384,1536]{1,0:T(8,128)(2,1)S(1)}, f32[384,1536]{1,0:T(8,128)}) fusion(f32[384,1536]{1,0:T(8,128)S(1)} %copy-done.3, f32[384,1536]{1,0:T(8,128)} %all-reduce.2.cloned.1.call-done), kind=kLoop, calls=%fused_computation.64 | loop fusion | flops 1179648 | bytes 8257536 | tf_op jit(solution)/shard_map/convert.1
  258.4 1.0 copy-done.5
  259.5 1.3 broadcast_in_dim.33
  260.8 8.0 %all-to-all-start.1 = ((bf16[16,32,1536]{2,1,0:T(8,128)(2,1)}), bf16[16,32,1536]{2,1,0:T(8,128)(2,1)S(1)}, u32[]{:S(2)}, u32[]{:S(2)}) async-start(bf16[16,32,1536]{2,1,0:T(8,128)(2,1)} %broadcast_in_dim.33), calls=%async_computation.1 | async-start | bytes 3145728 | tf_op jit(solution)/shard_map/all_to_all | solution.py:19
  268.8 0.2 all-gather.9.cloned.1.call-start
  269.0 0.0 copy-done.11
  269.0 2.1 convolution_convert_fusion.2
  271.1 0.0 all-gather.9.cloned.1.call-update
  271.1 0.0 copy-done.10
  271.2 28.6 %all-gather.9.cloned.1.call-done = bf16[1536,512]{1,0:T(8,128)(2,1)} async-done(((bf16[384,512]{1,0:T(8,128)(2,1)}), bf16[1536,512]{1,0:T(8,128)(2,1)}) %all-gather.9.cloned.1.call-update) | async-done | bytes 1572880 | tf_op jit(solution)/shard_map/all_gather | solution.py:27
  299.8 1.0 slice.17
  300.9 0.0 copy-start.4
  300.9 6.4 %all-to-all-done.1 = bf16[16,32,1536]{2,1,0:T(8,128)(2,1)S(1)} async-done(((bf16[16,32,1536]{2,1,0:T(8,128)(2,1)}), bf16[16,32,1536]{2,1,0:T(8,128)(2,1)S(1)}, u32[]{:S(2)}, u32[]{:S(2)}) %all-to-all-start.1) | async-done | bytes 1572896 | tf_op jit(solution)/shard_map/all_to_all | solution.py:19
  307.3 2.9 gather_fusion
  310.2 0.0 copy-done.12
  310.2 2.6 convolution_convert_fusion
  312.9 1.1 copy-done.2
  314.0 1.6 copy.18
  315.6 2.2 fusion.51
  317.8 0.0 copy-start.1
  317.8 3.8 %fusion.2 = f32[384,1536]{1,0:T(8,128)} fusion(f32[384,1536]{1,0:T(8,128)} %get-tuple-element.10, f32[384,1536]{1,0:T(8,128)S(1)} %fusion.51, s32[384]{0:T(512)S(1)} %add_select_fusion.1, s32[1536]{0:T(1024)S(1)} %add_select_fusion, s32[24,24]{1,0:T(8,128)S(1)} %copy-done.9), kind=kOutput, calls=%fused_computation.6 | convolution fusion | flops 29980224 | bytes 7087872 | tf_op jit(solution)/shard_map/rt,ts,cs->rc/dot_general | solution.py:83
  (22 shorter events, 0.1 us)
Async XLA Ops:
  7.2 1.2 copy-start
  7.2 3.8 %copy-start.6 = (bf16[1,8,32,1536]{3,2,1,0:T(8,128)(2,1)S(1)}, bf16[1,8,32,1536]{3,2,1,0:T(8,128)(2,1)}, u32[]{:S(2)}) copy-start(bf16[1,8,32,1536]{3,2,1,0:T(8,128)(2,1)} %param.13) | copy-start | bytes 2359300
  7.2 81.7 %all-gather.5.cloned.1.call-start = ((), (), s32[]{:S(2)}) async-start(), calls=%async_computation.2 | async-start | bytes 3932160 | tf_op jit(solution)/shard_map/all_gather | solution.py:67
  17.6 15.7 %copy-start.8 = (s32[1,8,512]{2,1,0:T(8,128)S(1)}, s32[1,8,512]{2,1,0:T(8,128)}, u32[]{:S(2)}) copy-start(s32[1,8,512]{2,1,0:T(8,128)} %param.16) | copy-start | bytes 49156
  23.3 32.7 %all-to-all-start = ((bf16[16,2,12288]{2,1,0:T(2,128)(2,1)}), bf16[16,2,12288]{2,1,0:T(2,128)(2,1)S(1)}, u32[]{:S(2)}, u32[]{:S(2)}) async-start(bf16[16,2,12288]{2,1,0:T(2,128)(2,1)} %reshape.121), calls=%async_computation | async-start | bytes 1572864 | tf_op jit(solution)/shard_map/all_to_all | solution.py:54
  33.3 128.5 %all-gather.7.cloned.1.call-start = ((), (), s32[]{:S(2)}) async-start(), calls=%async_computation.3 | async-start | bytes 13369344 | tf_op jit(solution)/shard_map/all_gather | solution.py:59
  88.8 166.1 %all-reduce.2.cloned.1.call-start = ((), (), s32[]{:S(2)}) async-start(), calls=%async_computation.4 | async-start | bytes 4718592 | tf_op jit(solution)/shard_map/psum | solution.py:72
  88.9 90.2 %copy-start.7 = (s32[1,8,24,24]{3,2,1,0:T(8,128)S(1)}, s32[1,8,24,24]{3,2,1,0:T(8,128)}, u32[]{:S(2)}) copy-start(s32[1,8,24,24]{3,2,1,0:T(8,128)} %param.17) | copy-start | bytes 55300
  188.7 66.2 %copy-start.3 = (f32[384,1536]{1,0:T(8,128)S(1)}, f32[384,1536]{1,0:T(8,128)}, u32[]{:S(2)}) copy-start(f32[384,1536]{1,0:T(8,128)} %param.11) | copy-start | bytes 7077892
  258.4 1.0 copy-start.5
  259.5 9.5 %copy-start.11 = (bf16[512,512]{1,0:T(8,128)(2,1)S(1)}, bf16[512,512]{1,0:T(8,128)(2,1)}, u32[]{:S(2)}) copy-start(bf16[512,512]{1,0:T(8,128)(2,1)} %param.18) | copy-start | bytes 1572868
  260.8 10.4 %copy-start.10 = (s32[512]{0:T(512)S(1)}, s32[512]{0:T(512)}, u32[]{:S(2)}) copy-start(s32[512]{0:T(512)} %param.20) | copy-start | bytes 6148
  260.8 46.5 %all-to-all-start.1 = ((bf16[16,32,1536]{2,1,0:T(8,128)(2,1)}), bf16[16,32,1536]{2,1,0:T(8,128)(2,1)S(1)}, u32[]{:S(2)}, u32[]{:S(2)}) async-start(bf16[16,32,1536]{2,1,0:T(8,128)(2,1)} %broadcast_in_dim.33), calls=%async_computation.1 | async-start | bytes 3145728 | tf_op jit(solution)/shard_map/all_to_all | solution.py:19
  268.8 31.1 %all-gather.9.cloned.1.call-start = ((), (), s32[]{:S(2)}) async-start(), calls=%async_computation.5 | async-start | bytes 1966080 | tf_op jit(solution)/shard_map/all_gather | solution.py:27
  300.9 14.7 %copy-start.4 = (bf16[384,512]{1,0:T(8,128)(2,1)}, bf16[384,512]{1,0:T(8,128)(2,1)S(1)}, u32[]{:S(2)}) copy-start(bf16[384,512]{1,0:T(8,128)(2,1)S(1)} %slice.17) | copy-start | bytes 1179652
  307.3 2.9 copy-start.12
  312.9 1.2 copy-start.2
  315.6 2.2 copy-start.9
  317.8 3.8 %copy-start.1 = (bf16[1,2,512,512]{3,2,1,0:T(8,128)(2,1)S(1)}, bf16[1,2,512,512]{3,2,1,0:T(8,128)(2,1)}, u32[]{:S(2)}) copy-start(bf16[1,2,512,512]{3,2,1,0:T(8,128)(2,1)} %param.14) | copy-start | bytes 3145732
Sparse Core Ops, SparseCore 0:
  11.1 45.6 all-gather.4
  88.9 72.8 all-gather.6
  188.8 66.0 all-reduce.1
  271.7 28.1 all-gather.8
where the time goes:
time: 329 us; the launch traced here: 328 us
  waiting for transfers between devices  197 us (60%)
  local copies, waits for them, and re-layouts  50.8 us (15%)
  matrix products  44.6 us (14%)
  starting transfers between devices  18.3 us (6%)
  between operations  14 us (4%)
  other arithmetic  3.63 us (1%)
    all_gather x1, waiting for transfers between devices, shards(): upper_all = lax.all_gather(finished, 'row', axis=2, tiled=True)  72.9 us
    psum x1, waiting for transfers between devices, shards(): total = lax.psum(contrib, 'layer')  66.2 us
    all_gather x1, waiting for transfers between devices, from_root(): lax.all_gather(x, axis)  28.6 us
    all_to_all x1, waiting for transfers between devices, shards(): lax.all_to_all(upper_local, 'row', split_axis=2, concat_axis=1, tiled=True)  22.6 us
    gather x1, local copies, waits for them, and re-layouts, shards(): jnp.take_along_axis(column_share, leaf_pivots[0][:, :, None], axis=1)  21.7 us
    unnamed x32, local copies, waits for them, and re-layouts  19.9 us
    dot_general x1, matrix products, shards(): jnp.einsum('mrw,mwc->mrc', lax.all_gather(own_lower, 'col', axis=0, tiled...  17.2 us
    all_to_all x1, starting transfers between devices, shards(): lax.all_to_all(upper_local, 'row', split_axis=2, concat_axis=1, tiled=True)  9.97 us
  transfers between devices with their start and end apart: 6, of which 5 were waited for; matrix products, arithmetic and copies ran while one was open for 15% of the time, Pallas kernels for 0%

commit v1 on v0

--- a/solution.py
+++ b/solution.py
@@ -6,6 +6,15 @@
 W = 512
 TB = 256
 NT = 24
+
+
+def sum_by_hops(x, mesh_axis):
+    size = lax.axis_size(mesh_axis)
+    summed, reach = (x, 1)
+    while reach < size:
+        summed = summed + lax.ppermute(summed, mesh_axis, [(i, i ^ reach) for i in range(size)])
+        reach = 2 * reach
+    return summed
 
 
 def joined_along(blocks, dim):
@@ -69,7 +78,7 @@
         preferred_element_type=jnp.float32,
     )
     contrib = jnp.sum(masks * products, axis=0)
-    total = lax.psum(contrib, "layer")
+    total = sum_by_hops(contrib, "layer")
     a_sum = ancestor + total
     local_pivot = a_sum[:panel_rows].astype(jnp.bfloat16)
     gathered = gathered_copies(local_pivot, "row", 0)

time: 329 us -> 367 us (1.12)
  waiting for transfers between devices: 197 us -> 233 us
    ppermute x0 -> x2, waiting for transfers between devices: none -> 102 us  [sum_by_hops(): lax.ppermute(summed, mesh_axis, [(i, i ^ reach) for i in range(size)])]
    psum x1 -> x0, waiting for transfers between devices: 66.2 us -> none  [shards(): total = lax.psum(contrib, 'layer')]
    ppermute x0 -> x2, starting transfers between devices: none -> 4.29 us  [sum_by_hops(): lax.ppermute(summed, mesh_axis, [(i, i ^ reach) for i in range(size)])]
    unnamed x32 -> x38, local copies, waits for them, and re-layouts: 19.9 us -> 20.6 us
  transfers between devices with their start and end apart: 6 -> 7, of which waited for: 5 -> 6; matrix products, arithmetic and copies ran while one was open for 15% -> 13% of each run, Pallas kernels for 0% -> 0%
where the time goes in v1:
time: 367 us; the launch traced here: 366 us
  waiting for transfers between devices  233 us (63%)
  local copies, waits for them, and re-layouts  51.4 us (14%)
  matrix products  46.3 us (13%)
  starting transfers between devices  20.7 us (6%)
  between operations  14 us (4%)
    ppermute x2, waiting for transfers between devices, sum_by_hops(): lax.ppermute(summed, mesh_axis, [(i, i ^ reach) for i in range(size)])  102 us
    all_gather x1, waiting for transfers between devices, shards(): upper_all = lax.all_gather(finished, 'row', axis=2, tiled=True)  73 us
    all_gather x1, waiting for transfers between devices, from_root(): lax.all_gather(x, axis)  30.6 us
    all_to_all x1, waiting for transfers between devices, shards(): lax.all_to_all(upper_local, 'row', split_axis=2, concat_axis=1, tiled=True)  22.6 us
    gather x1, local copies, waits for them, and re-layouts, shards(): jnp.take_along_axis(column_share, leaf_pivots[0][:, :, None], axis=1)  21.7 us
    unnamed x38, local copies, waits for them, and re-layouts  20.6 us
    dot_general x1, matrix products, shards(): jnp.einsum('mrw,mwc->mrc', lax.all_gather(own_lower, 'col', axis=0, tiled...  17.2 us
    all_to_all x1, starting transfers between devices, shards(): lax.all_to_all(upper_local, 'row', split_axis=2, concat_axis=1, tiled=True)  9.97 us
  transfers between devices with their start and end apart: 7, of which 6 were waited for; matrix products, arithmetic and copies ran while one was open for 13% of the time, Pallas kernels for 0%

profile of v1, /device:TPU:1, one launch (start us, length us, event | category | flops | bytes accessed | tf_op | source)
XLA Modules:
  0.0 366.4 jit_solution(3402713762394614920)
XLA Ops:
  7.2 0.0 copy-start
  7.2 0.0 copy-start.9
  7.2 0.0 all-gather.5.cloned.1.call-start
  7.2 1.2 copy-done
  8.4 2.6 convolution_convert_fusion.1
  11.0 0.0 all-gather.5.cloned.1.call-update
  11.0 0.0 copy-done.9
  11.0 3.5 copy.16
  14.5 3.1 bitcast_bitcast_fusion
  17.6 5.7 %reshape.121 = bf16[16,2,12288]{2,1,0:T(2,128)(2,1)} reshape(bf16[1536,8,32]{2,1,0:T(8,128)(2,1)} %bitcast_bitcast_fusion) | data formatting | bytes 1572864
  23.4 10.0 %all-to-all-start = ((bf16[16,2,12288]{2,1,0:T(2,128)(2,1)}), bf16[16,2,12288]{2,1,0:T(2,128)(2,1)S(1)}, u32[]{:S(2)}, u32[]{:S(2)}) async-start(bf16[16,2,12288]{2,1,0:T(2,128)(2,1)} %reshape.121), calls=%async_computation | async-start | bytes 1572864 | tf_op jit(solution)/shard_map/all_to_all | solution.py:63
  33.3 0.0 all-gather.7.cloned.1.call-start
  33.4 0.0 copy-done.11
  33.4 22.6 %all-to-all-done = bf16[16,2,12288]{2,1,0:T(2,128)(2,1)S(1)} async-done(((bf16[16,2,12288]{2,1,0:T(2,128)(2,1)}), bf16[16,2,12288]{2,1,0:T(2,128)(2,1)S(1)}, u32[]{:S(2)}, u32[]{:S(2)}) %all-to-all-start) | async-done | bytes 786464 | tf_op jit(solution)/shard_map/all_to_all | solution.py:63
  56.0 2.7 reshape.122
  58.7 3.9 %copy.17 = bf16[8,32,16,96]{3,1,2,0:T(8,128)(2,1)S(1)} copy(bf16[8,32,16,96]{1,0,3,2:T(8,128)(2,1)} %bitcast.62) | data formatting | bytes 1572864 | tf_op jit(solution)/shard_map/all_to_all | solution.py:63
  62.6 21.7 %gather_fusion.1 = bf16[4096,96]{1,0:T(8,128)(2,1)S(1)} fusion(bf16[8,512,96]{2,1,0:T(8,128)(2,1)S(1)} %bitcast.61, s32[4096]{0:T(1024)S(1)} %bitcast.59), kind=kCustom, calls=%fused_computation.1 | custom fusion | bytes 1605632 | tf_op jit(solution)/shard_map/jit(take_along_axis)/gather | solution.py:64
  84.3 4.5 %fusion.8 = bf16[8,512,96]{1,2,0:T(8,128)(2,1)} fusion(bf16[1,8,512,512]{3,2,1,0:T(8,128)(2,1)} %param.15, bf16[8,512,96]{2,1,0:T(8,128)(2,1)S(1)} %bitcast.64, pred[8,512]{1,0:T(8,128)(4,1)S(1)} %compare_and_fusion), kind=kOutput, calls=%fused_computation.13 | convolution fusion | flops 403439616 | bytes 5771264 | tf_op jit(solution)/shard_map/kij,kjc->kic/dot_general | solution.py:65
  88.8 0.0 all-gather.7.cloned.1.call-update
  88.8 0.0 copy-start.10
  88.9 0.0 all-gather.5.cloned.1.call-done
  88.9 73.0 %all-gather.7.cloned.1.call-done = bf16[8,512,1536]{1,2,0:T(8,128)(2,1)} async-done(((bf16[8,512,96]{1,2,0:T(8,128)(2,1)}), bf16[8,512,1536]{1,2,0:T(8,128)(2,1)}) %all-gather.7.cloned.1.call-update) | async-done | bytes 12582928 | tf_op jit(solution)/shard_map/all_gather | solution.py:68
  161.9 17.2 %fusion.50 = f32[8,384,1536]{2,1,0:T(8,128)} fusion(bf16[8,384,512]{2,1,0:T(8,128)(2,1)} %all-gather.5.cloned.1.call-done, bf16[8,512,1536]{1,2,0:T(8,128)(2,1)} %all-gather.7.cloned.1.call-done), kind=kOutput, calls=%fused_computation.67 | convolution fusion | flops 4831838208 | bytes 34603008 | tf_op jit(solution)/shard_map/mrw,mwc->mrc/dot_general | solution.py:74
  179.1 8.2 %multiply_reduce_fusion = f32[384,1536]{1,0:T(8,128)S(1)} fusion(f32[8,384,1536]{2,1,0:T(8,128)} %fusion.50, s32[1,8,24,24]{3,2,1,0:T(8,128)S(1)} %copy-done.10, s32[384]{0:T(512)S(1)} %add_select_fusion.1, s32[1536]{0:T(1024)S(1)} %add_select_fusion), kind=kOutput, calls=%fused_computation.2 | convolution fusion | flops 238929408 | bytes 21259776 | tf_op jit(solution)/shard_map/rt,mts,cs->mrc/dot_general | solution.py:73
  187.3 0.0 copy-start.4
  187.3 1.3 collective-permute-start
  188.6 51.3 %collective-permute-done = f32[384,1536]{1,0:T(8,128)S(1)} collective-permute-done((f32[384,1536]{1,0:T(8,128)S(1)}, f32[384,1536]{1,0:T(8,128)S(1)}, u32[]{:S(2)}, u32[]{:S(2)}) %collective-permute-start) | collective-permute-done | bytes 2359328 | tf_op jit(solution)/shard_map/ppermute | solution.py:15
  239.9 0.4 add.79
  240.3 3.0 collective-permute-start.1
  243.3 50.5 %collective-permute-done.1 = f32[384,1536]{1,0:T(8,128)S(1)} collective-permute-done((f32[384,1536]{1,0:T(8,128)S(1)}, f32[384,1536]{1,0:T(8,128)S(1)}, u32[]{:S(2)}, u32[]{:S(2)}) %collective-permute-start.1) | collective-permute-done | bytes 2359328 | tf_op jit(solution)/shard_map/ppermute | solution.py:15
  293.8 0.8 fusion.49
  294.6 0.6 copy-done.5
  295.2 1.0 copy-done.8
  296.2 1.3 broadcast_in_dim.33
  297.5 6.4 %all-to-all-start.1 = ((bf16[16,32,1536]{2,1,0:T(8,128)(2,1)}), bf16[16,32,1536]{2,1,0:T(8,128)(2,1)S(1)}, u32[]{:S(2)}, u32[]{:S(2)}) async-start(bf16[16,32,1536]{2,1,0:T(8,128)(2,1)} %broadcast_in_dim.33), calls=%async_computation.1 | async-start | bytes 3145728 | tf_op jit(solution)/shard_map/all_to_all | solution.py:28
  303.9 0.0 all-gather.9.cloned.1.call-start
  304.0 2.1 convolution_convert_fusion.2
  306.1 0.0 all-gather.9.cloned.1.call-update
  306.1 30.6 %all-gather.9.cloned.1.call-done = bf16[1536,512]{1,0:T(8,128)(2,1)} async-done(((bf16[384,512]{1,0:T(8,128)(2,1)}), bf16[1536,512]{1,0:T(8,128)(2,1)}) %all-gather.9.cloned.1.call-update) | async-done | bytes 1572880 | tf_op jit(solution)/shard_map/all_gather | solution.py:36
  336.8 1.0 slice.17
  337.8 0.0 copy-start.7
  337.8 4.6 %all-to-all-done.1 = bf16[16,32,1536]{2,1,0:T(8,128)(2,1)S(1)} async-done(((bf16[16,32,1536]{2,1,0:T(8,128)(2,1)}), bf16[16,32,1536]{2,1,0:T(8,128)(2,1)S(1)}, u32[]{:S(2)}, u32[]{:S(2)}) %all-to-all-start.1) | async-done | bytes 1572896 | tf_op jit(solution)/shard_map/all_to_all | solution.py:28
  342.4 2.9 gather_fusion
  345.4 2.6 convolution_convert_fusion
  348.0 1.2 copy-done.6
  349.2 1.6 copy.18
  350.8 3.8 %fusion.51 = f32[384,1536]{1,0:T(8,128)} fusion(bf16[384,512]{1,0:T(8,128)(2,1)S(1)} %slice.17, bf16[1536,512]{1,0:T(8,128)(2,1)} %copy-done.6), kind=kOutput, calls=%fused_computation.68 | convolution fusion | flops 603979776 | bytes 4325376 | tf_op jit(solution)/shard_map/dot_general | solution.py:93
  354.5 5.3 %fusion.2 = f32[384,1536]{1,0:T(8,128)} fusion(f32[384,1536]{1,0:T(8,128)} %fusion.51, s32[384]{0:T(512)S(1)} %add_select_fusion.1, s32[1536]{0:T(1024)S(1)} %add_select_fusion, s32[24,24]{1,0:T(8,128)S(1)} %copy-done.12, f32[384,1536]{1,0:T(8,128)} %param.11, f32[384,1536]{1,0:T(8,128)S(1)} %copy-done.3, f32[384,1536]{1,0:T(8,128)} %copy-done.5), kind=kOutput, calls=%fused_computation.6 | convolution fusion | flops 31159872 | bytes 11806464 | tf_op jit(solution)/shard_map/rt,ts,cs->rc/dot_general | solution.py:92
  (30 shorter events, 0.1 us)
Async XLA Ops:
  7.2 1.2 copy-start
  7.2 3.8 %copy-start.9 = (bf16[1,8,32,1536]{3,2,1,0:T(8,128)(2,1)S(1)}, bf16[1,8,32,1536]{3,2,1,0:T(8,128)(2,1)}, u32[]{:S(2)}) copy-start(bf16[1,8,32,1536]{3,2,1,0:T(8,128)(2,1)} %param.13) | copy-start | bytes 2359300
  7.2 81.7 %all-gather.5.cloned.1.call-start = ((), (), s32[]{:S(2)}) async-start(), calls=%async_computation.2 | async-start | bytes 3932160 | tf_op jit(solution)/shard_map/all_gather | solution.py:76
  17.6 15.7 %copy-start.11 = (s32[1,8,512]{2,1,0:T(8,128)S(1)}, s32[1,8,512]{2,1,0:T(8,128)}, u32[]{:S(2)}) copy-start(s32[1,8,512]{2,1,0:T(8,128)} %param.16) | copy-start | bytes 49156
  23.4 32.7 %all-to-all-start = ((bf16[16,2,12288]{2,1,0:T(2,128)(2,1)}), bf16[16,2,12288]{2,1,0:T(2,128)(2,1)S(1)}, u32[]{:S(2)}, u32[]{:S(2)}) async-start(bf16[16,2,12288]{2,1,0:T(2,128)(2,1)} %reshape.121), calls=%async_computation | async-start | bytes 1572864 | tf_op jit(solution)/shard_map/all_to_all | solution.py:63
  33.3 128.5 %all-gather.7.cloned.1.call-start = ((), (), s32[]{:S(2)}) async-start(), calls=%async_computation.3 | async-start | bytes 13369344 | tf_op jit(solution)/shard_map/all_gather | solution.py:68
  88.8 90.2 %copy-start.10 = (s32[1,8,24,24]{3,2,1,0:T(8,128)S(1)}, s32[1,8,24,24]{3,2,1,0:T(8,128)}, u32[]{:S(2)}) copy-start(s32[1,8,24,24]{3,2,1,0:T(8,128)} %param.17) | copy-start | bytes 55300
  187.3 106.5 %copy-start.4 = (f32[384,1536]{1,0:T(8,128)S(1)}, f32[384,1536]{1,0:T(8,128)}, u32[]{:S(2)}) copy-start(f32[384,1536]{1,0:T(8,128)} %param.11) | copy-start | bytes 7077892
  187.3 52.6 %collective-permute-start = (f32[384,1536]{1,0:T(8,128)S(1)}, f32[384,1536]{1,0:T(8,128)S(1)}, u32[]{:S(2)}, u32[]{:S(2)}) collective-permute-start(f32[384,1536]{1,0:T(8,128)S(1)} %multiply_reduce_fusion), channel_id=1, source_target_pairs={{0,64},{64,0},{128,192},{192,128},{1,65},{65,1},{129,193},{193,129... | collective-permute-start | bytes 7077896 | tf_op jit(solution)/shard_map/ppermute | solution.py:15
  240.3 54.3 %copy-start.2 = (f32[384,1536]{1,0:T(8,128)}, f32[384,1536]{1,0:T(8,128)S(1)}, u32[]{:S(2)}) copy-start(f32[384,1536]{1,0:T(8,128)S(1)} %add.79) | copy-start | bytes 7077892
  240.3 53.5 %collective-permute-start.1 = (f32[384,1536]{1,0:T(8,128)S(1)}, f32[384,1536]{1,0:T(8,128)S(1)}, u32[]{:S(2)}, u32[]{:S(2)}) collective-permute-start(f32[384,1536]{1,0:T(8,128)S(1)} %add.79), channel_id=1, source_target_pairs={{0,128},{64,192},{128,0},{192,64},{1,129},{65,193},{129,1},{193,65... | collective-permute-start | bytes 7077896 | tf_op jit(solution)/shard_map/ppermute | solution.py:15
  293.8 1.4 copy-start.5
  295.2 1.0 copy-start.8
  296.2 7.7 %copy-start.14 = (bf16[512,512]{1,0:T(8,128)(2,1)S(1)}, bf16[512,512]{1,0:T(8,128)(2,1)}, u32[]{:S(2)}) copy-start(bf16[512,512]{1,0:T(8,128)(2,1)} %param.18) | copy-start | bytes 1572868
  297.5 8.6 %copy-start.13 = (s32[512]{0:T(512)S(1)}, s32[512]{0:T(512)}, u32[]{:S(2)}) copy-start(s32[512]{0:T(512)} %param.20) | copy-start | bytes 6148
  297.5 44.9 %all-to-all-start.1 = ((bf16[16,32,1536]{2,1,0:T(8,128)(2,1)}), bf16[16,32,1536]{2,1,0:T(8,128)(2,1)S(1)}, u32[]{:S(2)}, u32[]{:S(2)}) async-start(bf16[16,32,1536]{2,1,0:T(8,128)(2,1)} %broadcast_in_dim.33), calls=%async_computation.1 | async-start | bytes 3145728 | tf_op jit(solution)/shard_map/all_to_all | solution.py:28
  303.9 32.9 %all-gather.9.cloned.1.call-start = ((), (), s32[]{:S(2)}) async-start(), calls=%async_computation.4 | async-start | bytes 1966080 | tf_op jit(solution)/shard_map/all_gather | solution.py:36
  337.8 13.0 %copy-start.7 = (bf16[384,512]{1,0:T(8,128)(2,1)}, bf16[384,512]{1,0:T(8,128)(2,1)S(1)}, u32[]{:S(2)}) copy-start(bf16[384,512]{1,0:T(8,128)(2,1)S(1)} %slice.17) | copy-start | bytes 1179652
  342.4 2.9 copy-start.15
  348.0 1.2 copy-start.6
  350.8 3.8 %copy-start.3 = (f32[384,1536]{1,0:T(8,128)S(1)}, f32[384,1536]{1,0:T(8,128)}, u32[]{:S(2)}) copy-start(f32[384,1536]{1,0:T(8,128)} %copy-done.2) | copy-start | bytes 7077892
  350.8 3.8 %copy-start.12 = (s32[24,24]{1,0:T(8,128)S(1)}, s32[24,24]{1,0:T(8,128)}, u32[]{:S(2)}) copy-start(s32[24,24]{1,0:T(8,128)} %param.21) | copy-start | bytes 6916
  354.5 5.3 %copy-start.1 = (bf16[1,2,512,512]{3,2,1,0:T(8,128)(2,1)S(1)}, bf16[1,2,512,512]{3,2,1,0:T(8,128)(2,1)}, u32[]{:S(2)}) copy-start(bf16[1,2,512,512]{3,2,1,0:T(8,128)(2,1)} %param.14) | copy-start | bytes 3145732
Sparse Core Ops, SparseCore 0:
  11.1 45.6 all-gather.4
  88.9 72.8 all-gather.6
  307.1 29.6 all-gather.8
